TPU v7x, 32 devices: a whole 2x2x4 slice. The times are simulated.
32 devices in a mesh: grp: 8 (over z, y), ep: 4 (over x, core).
Axes of the slice: x: 2, y: 2, z: 4, core: 2. Of those that a mesh axis runs over, the one named last changes fastest.
Arguments:
- tokens: bfloat16 [6144, 4096], P(('grp', 'ep')), may hold values from -6 to 6
- expert_ids: int32 [6144, 8], P(('grp', 'ep')), may hold values from 0 to 127, all different within a row; in each aligned block of 192 rows (0 to 191, 192 to 383, ...) at most 24 rows name the same one
- gate_probs: float32 [6144, 8], P(('grp', 'ep')), may hold values from 0.02 to 0.25
- placement: int32 [8, 1], P('grp'), may hold values from 0 to 1
- gate_weight: bfloat16 [8, 4096, 768], P('grp', None, 'ep'), may hold values from -0.09375 to 0.09375
- up_weight: bfloat16 [8, 4096, 768], P('grp', None, 'ep'), may hold values from -0.09375 to 0.09375
- down_weight: bfloat16 [8, 768, 4096], P('grp', 'ep'), may hold values from -0.21875 to 0.21875
- out_grad: bfloat16 [6144, 4096], P(('grp', 'ep')), may hold values from -6 to 6
- moment_first: float32 [2, 768, 4096], P(None, 'ep', 'grp'), may hold values from -2 to 2
- moment_second: float32 [2, 768, 4096], P(None, 'ep', 'grp'), may hold values from 0.01 to 1
Outputs:
- token_grad: bfloat16 [6144, 4096], P(('grp', 'ep'))
- step_dir: bfloat16 [8, 768, 4096], P('grp', 'ep')
- new_first: float32 [2, 768, 4096], P(None, 'ep', 'grp')
- new_second: float32 [2, 768, 4096], P(None, 'ep', 'grp')
Inputs may be any that keep to these rules, and one draw needn't show every extreme that they name: `expert_ids`: each row names 8 different experts. In the rows of one device no expert is named more than 24 times, a bound that some block reaches. Group g holds expert placement[g, s] + s in its slot s.
All inputs are finite; a program needn't handle non-finite values.
Results may differ from a plain program's by a relative error of at most 0.015.
Values may be sent and summed in bfloat16 or wider, within the bound.
No kernel may reach another device: no remote copies, remote signals or barrier semaphores. Data moves between devices by JAX's collectives and lax.ppermute only.
A program may use at most 128 MiB of HBM per device.

v0:
```python
import math
import jax
import jax.numpy as jnp
from jax import lax
from jax.sharding import PartitionSpec as P

QUARTERS = 4
CANDS = 2
CAP = 24
beta_one = 0.9
beta_two = 0.999
adam_eps = 1e-08
first_fix = 1.0 - math.exp(1000.0 * math.log(0.9))
second_fix = 1.0 - math.exp(1000.0 * math.log(0.999))


def moments(gradient, first_moment, second):
    new_first = beta_one * first_moment + (1.0 - beta_one) * gradient
    new_second = beta_two * second + (1.0 - beta_two) * gradient * gradient
    return (new_first, new_second)


def direction(new_first, new_second):
    return new_first / first_fix / (jnp.sqrt(new_second / second_fix) + adam_eps)


def body(
    tokens,
    expert_ids,
    gate_probs,
    placement,
    gate_weight,
    up_weight,
    down_weight,
    out_grad,
    moment_first,
    moment_second,
):
    num_ep = lax.axis_size("ep")
    slot_count = num_ep // QUARTERS
    tok_count = tokens.shape[0]
    width = tokens.shape[1]
    held_ids = placement[0] * slot_count + jnp.arange(slot_count, dtype=jnp.int32)
    matches = expert_ids[:, :, None] == held_ids[None, None, :]
    hit_rows = jnp.any(matches, axis=1)
    coeffs = jnp.sum(jnp.where(matches, gate_probs[:, :, None], jnp.float32(0.0)), axis=1)
    ranking = jnp.cumsum(hit_rows.astype(jnp.int32), axis=0) - 1
    select_mask = hit_rows.T[:, None, :] & (
        ranking.T[:, None, :] == jnp.arange(CAP, dtype=jnp.int32)[None, :, None]
    )
    select_flat = select_mask.reshape(slot_count * CAP, tok_count).astype(jnp.bfloat16)
    send_tokens = jnp.dot(select_flat, tokens, preferred_element_type=jnp.float32).astype(
        jnp.bfloat16
    )
    send_grads = jnp.dot(select_flat, out_grad, preferred_element_type=jnp.float32).astype(
        jnp.bfloat16
    )
    send_coeffs = jnp.sum(select_mask.astype(jnp.float32) * coeffs.T[:, None, :], axis=2)

    def spread(source):
        shaped = source.reshape(slot_count, 1, CAP, width)
        return jnp.broadcast_to(shaped, (slot_count, QUARTERS, CAP, width)).reshape(
            num_ep, CAP, width
        )

    coeff_spread = jnp.broadcast_to(send_coeffs[:, None, :], (slot_count, QUARTERS, CAP)).reshape(
        num_ep, CAP
    )
    w_gate = gate_weight[0]
    w_up = up_weight[0]
    w_down = down_weight[0]
    recv_tokens, recv_grads, recv_coeffs = (
        lax.all_to_all(spread(send_tokens), "ep", split_axis=0, concat_axis=0, tiled=True),
        lax.all_to_all(spread(send_grads), "ep", split_axis=0, concat_axis=0, tiled=True),
        lax.all_to_all(
            coeff_spread.astype(jnp.bfloat16), "ep", split_axis=0, concat_axis=0, tiled=True
        ).astype(coeff_spread.dtype),
    )
    in_rows = recv_tokens.reshape(num_ep * CAP, width)
    pre_gate = jnp.dot(in_rows, w_gate, preferred_element_type=jnp.float32)
    pre_up = jnp.dot(in_rows, w_up, preferred_element_type=jnp.float32)
    sigmoid_gate = jax.nn.sigmoid(pre_gate)
    activated = pre_gate * sigmoid_gate
    hidden = (activated * pre_up).astype(jnp.bfloat16)
    pre_gate, pre_up, sigmoid_gate, activated, hidden = (
        pre_gate,
        pre_up,
        sigmoid_gate,
        activated,
        hidden,
    )
    scaled = (
        recv_coeffs.reshape(num_ep * CAP)[:, None]
        * recv_grads.reshape(num_ep * CAP, width).astype(jnp.float32)
    ).astype(jnp.bfloat16)
    d_hidden = jnp.einsum("rd,hd->rh", scaled, w_down, preferred_element_type=jnp.float32)
    weight_grad = jnp.einsum("rh,rd->hd", hidden, scaled, preferred_element_type=jnp.float32)
    d_gate = (d_hidden * pre_up * sigmoid_gate * (1.0 + pre_gate * (1.0 - sigmoid_gate))).astype(
        jnp.bfloat16
    )
    d_up = (d_hidden * activated).astype(jnp.bfloat16)
    partial_value = jnp.einsum("rh,dh->rd", d_gate, w_gate, preferred_element_type=jnp.float32)
    partial_value = (
        partial_value + jnp.einsum("rh,dh->rd", d_up, w_up, preferred_element_type=jnp.float32)
    ).astype(jnp.bfloat16)
    returned = lax.all_to_all(
        partial_value.reshape(num_ep, CAP, width), "ep", split_axis=0, concat_axis=0, tiled=True
    )
    combine = jnp.broadcast_to(
        select_mask.reshape(slot_count, 1, CAP, tok_count), (slot_count, QUARTERS, CAP, tok_count)
    )
    combine = combine.reshape(num_ep * CAP, tok_count).astype(jnp.bfloat16)
    token_grad = jnp.einsum(
        "kt,kd->td",
        combine,
        returned.reshape(num_ep * CAP, width),
        preferred_element_type=jnp.float32,
    ).astype(jnp.bfloat16)
    ep_index = lax.axis_index("ep")
    my_cand = lax.dynamic_index_in_dim(placement[0], ep_index // QUARTERS, 0, keepdims=False)
    cand_mask = (jnp.arange(CANDS, dtype=jnp.int32) == my_cand).astype(jnp.float32)
    cand_grads = cand_mask[:, None, None] * weight_grad[None]
    shares = lax.psum_scatter(
        cand_grads.astype(jnp.bfloat16), "grp", scatter_dimension=2, tiled=True
    ).astype(jnp.float32)
    new_first, new_second = moments(shares, moment_first, moment_second)
    dir_share = direction(new_first, new_second).astype(jnp.bfloat16)
    all_dirs = lax.all_gather(dir_share, "grp", axis=2, tiled=True)
    step_dir = lax.dynamic_index_in_dim(all_dirs, my_cand, 0, keepdims=True)
    return (token_grad, step_dir, new_first, new_second)


def solution(mesh):
    return jax.shard_map(
        body,
        mesh=mesh,
        in_specs=(
            P(("grp", "ep"), None),
            P(("grp", "ep"), None),
            P(("grp", "ep"), None),
            P("grp", None),
            P("grp", None, "ep"),
            P("grp", None, "ep"),
            P("grp", "ep", None),
            P(("grp", "ep"), None),
            P(None, "ep", "grp"),
            P(None, "ep", "grp"),
        ),
        out_specs=(
            P(("grp", "ep"), None),
            P("grp", "ep", None),
            P(None, "ep", "grp"),
            P(None, "ep", "grp"),
        ),
        check_vma=False,
    )
```

profile of v0, /device:TPU:0, one launch (start us, length us, event | category | flops | bytes accessed | tf_op | source)
XLA Modules:
  0.0 203.4 jit_solution(15359408205191118188)
XLA Ops:
  7.2 0.0 copy-start
  7.9 0.7 select_reduce_fusion.1
  8.7 0.3 reduce-window.6
  9.0 0.2 slice_reduce_fusion
  9.2 0.2 reduce-window.9
  9.4 0.1 broadcast.180
  9.5 0.1 select_reduce_fusion
  9.6 0.6 reshape.302
  10.2 4.2 %all-to-all-start = ((bf16[4,1,24]{2,1,0:T(2,128)(2,1)}), bf16[4,1,24]{2,1,0:T(2,128)(2,1)S(1)}, u32[]{:S(2)}, u32[]{:S(2)}) async-start(bf16[4,1,24]{2,1,0:T(2,128)(2,1)} %reshape.302), calls=%async_computation | async-start | bytes 4096 | tf_op jit(solution)/shard_map/all_to_all | solution.py:75
  14.4 1.7 convolution_convert_fusion
  16.2 2.0 all-to-all-done
  18.1 0.9 reshape.304
  19.1 3.5 %all-to-all-start.2 = ((bf16[4,24,4096]{2,1,0:T(8,128)(2,1)}), bf16[4,24,4096]{2,1,0:T(8,128)(2,1)S(1)}, u32[]{:S(2)}, u32[]{:S(2)}) async-start(bf16[4,24,4096]{2,1,0:T(8,128)(2,1)} %reshape.304), calls=%async_computation.2 | async-start | bytes 1572864 | tf_op jit(solution)/shard_map/all_to_all | solution.py:73
  22.6 1.7 convolution_convert_fusion.1
  24.3 9.9 %all-to-all-done.2 = bf16[4,24,4096]{2,1,0:T(8,128)(2,1)S(1)} async-done(((bf16[4,24,4096]{2,1,0:T(8,128)(2,1)}), bf16[4,24,4096]{2,1,0:T(8,128)(2,1)S(1)}, u32[]{:S(2)}, u32[]{:S(2)}) %all-to-all-start.2) | async-done | bytes 786464 | tf_op jit(solution)/shard_map/all_to_all | solution.py:73
  34.2 0.9 reshape.303
  35.1 3.5 %all-to-all-start.1 = ((bf16[4,24,4096]{2,1,0:T(8,128)(2,1)}), bf16[4,24,4096]{2,1,0:T(8,128)(2,1)S(1)}, u32[]{:S(2)}, u32[]{:S(2)}) async-start(bf16[4,24,4096]{2,1,0:T(8,128)(2,1)} %reshape.303), calls=%async_computation.1 | async-start | bytes 1572864 | tf_op jit(solution)/shard_map/all_to_all | solution.py:74
  38.6 0.0 reduce-scatter.2.cloned.1.call-start
  38.7 0.1 reshape.309
  38.8 0.0 copy-start.1
  38.8 0.0 copy-done
  38.8 0.6 fusion.5
  39.4 0.8 copy-done.1
  40.2 0.6 fusion.8
  40.8 9.4 %all-to-all-done.1 = bf16[4,24,4096]{2,1,0:T(8,128)(2,1)S(1)} async-done(((bf16[4,24,4096]{2,1,0:T(8,128)(2,1)}), bf16[4,24,4096]{2,1,0:T(8,128)(2,1)S(1)}, u32[]{:S(2)}, u32[]{:S(2)}) %all-to-all-start.1) | async-done | bytes 786464 | tf_op jit(solution)/shard_map/all_to_all | solution.py:74
  50.2 0.2 fusion.2
  50.4 0.6 fusion.15
  51.0 2.2 %multiply_convert_fusion = bf16[2,192,4096]{2,1,0:T(8,128)(2,1)} fusion(f32[192,4096]{1,0:T(8,128)S(1)} %fusion.15, f32[2]{0:T(128)S(1)} %compare_convert_fusion), kind=kLoop, calls=%fused_computation | loop fusion | flops 3145728 | bytes 6291464 | tf_op jit(solution)/shard_map/convert_element_type | solution.py:124
  53.3 0.0 copy-start.4
  53.3 0.0 reduce-scatter.2.cloned.1.call-update
  53.3 0.0 all-gather.2.cloned.1.call-start
  53.4 75.7 %reduce-scatter.2.cloned.1.call-done = bf16[2,192,512]{2,1,0:T(8,128)(2,1)} async-done(((bf16[2,192,4096]{2,1,0:T(8,128)(2,1)}), bf16[2,192,512]{2,1,0:T(8,128)(2,1)}) %reduce-scatter.2.cloned.1.call-update) | async-done | bytes 393232 | tf_op jit(solution)/shard_map/reduce_scatter | solution.py:123
  129.0 0.0 copy-done.4
  129.0 2.8 %divide_convert_fusion = (bf16[2,192,512]{2,1,0:T(8,128)(2,1)}, f32[2,192,512]{2,1,0:T(8,128)}, f32[2,192,512]{2,1,0:T(8,128)}) fusion(bf16[2,192,512]{2,1,0:T(8,128)(2,1)} %reduce-scatter.2.cloned.1.call-done, f32[2,192,512]{2,1,0:T(8,128)S(1)} %copy-done.4, f32[2,192,512]{2,1,0:T(8,128)} %param.18), kind=kLoop, calls=%fused_computation.23 | loop fusion | flops 2359296 | bytes 3932160 | tf_op jit(solution)/shard_map/convert_element_type | solution.py:127
  131.9 0.0 all-gather.2.cloned.1.call-update
  131.9 0.0 copy-start.3
  131.9 0.2 multiply_convert_fusion.1
  132.1 1.2 copy-done.3
  133.3 0.6 fusion.10
  134.0 0.0 copy-start.2
  134.0 0.4 fusion.3
  134.4 1.0 copy-done.2
  135.4 1.3 fusion.1
  136.6 3.5 %all-to-all-start.3 = ((bf16[4,24,4096]{2,1,0:T(8,128)(2,1)}), bf16[4,24,4096]{2,1,0:T(8,128)(2,1)S(1)}, u32[]{:S(2)}, u32[]{:S(2)}) async-start(bf16[4,24,4096]{2,1,0:T(8,128)(2,1)} %bitcast.12), calls=%async_computation.3 | async-start | bytes 1572864 | tf_op jit(solution)/shard_map/all_to_all | solution.py:106
  140.2 11.6 %all-to-all-done.3 = bf16[4,24,4096]{2,1,0:T(8,128)(2,1)S(1)} async-done(((bf16[4,24,4096]{2,1,0:T(8,128)(2,1)}), bf16[4,24,4096]{2,1,0:T(8,128)(2,1)S(1)}, u32[]{:S(2)}, u32[]{:S(2)}) %all-to-all-start.3) | async-done | bytes 786464 | tf_op jit(solution)/shard_map/all_to_all | solution.py:106
  151.8 1.8 fusion
  153.5 40.3 %all-gather.2.cloned.1.call-done = bf16[2,192,4096]{2,1,0:T(8,128)(2,1)} async-done(((bf16[2,192,512]{2,1,0:T(8,128)(2,1)}), bf16[2,192,4096]{2,1,0:T(8,128)(2,1)}) %all-gather.2.cloned.1.call-update) | async-done | bytes 3145744 | tf_op jit(solution)/shard_map/all_gather | solution.py:128
  193.8 2.7 %constant_dynamic-slice_fusion = bf16[1,192,4096]{2,1,0:T(8,128)(2,1)} fusion(bf16[2,192,4096]{2,1,0:T(8,128)(2,1)} %all-gather.2.cloned.1.call-done, s32[]{:T(128)S(6)} %select_n.15), kind=kLoop, calls=%fused_computation.45 | loop fusion | bytes 3145732 | tf_op jit(solution)/shard_map/jit(dynamic_index_in_dim)/dynamic_slice | solution.py:129
  (9 shorter events, 0.1 us)
Async XLA Ops:
  7.2 31.6 %copy-start = (bf16[1,4096,192]{1,2,0:T(8,128)(2,1)S(1)}, bf16[1,4096,192]{1,2,0:T(8,128)(2,1)}, u32[]{:S(2)}) copy-start(bf16[1,4096,192]{1,2,0:T(8,128)(2,1)} %param.14) | copy-start | bytes 4718596
  10.2 7.9 %all-to-all-start = ((bf16[4,1,24]{2,1,0:T(2,128)(2,1)}), bf16[4,1,24]{2,1,0:T(2,128)(2,1)S(1)}, u32[]{:S(2)}, u32[]{:S(2)}) async-start(bf16[4,1,24]{2,1,0:T(2,128)(2,1)} %reshape.302), calls=%async_computation | async-start | bytes 4096 | tf_op jit(solution)/shard_map/all_to_all | solution.py:75
  19.1 15.1 %all-to-all-start.2 = ((bf16[4,24,4096]{2,1,0:T(8,128)(2,1)}), bf16[4,24,4096]{2,1,0:T(8,128)(2,1)S(1)}, u32[]{:S(2)}, u32[]{:S(2)}) async-start(bf16[4,24,4096]{2,1,0:T(8,128)(2,1)} %reshape.304), calls=%async_computation.2 | async-start | bytes 1572864 | tf_op jit(solution)/shard_map/all_to_all | solution.py:73
  35.1 15.1 %all-to-all-start.1 = ((bf16[4,24,4096]{2,1,0:T(8,128)(2,1)}), bf16[4,24,4096]{2,1,0:T(8,128)(2,1)S(1)}, u32[]{:S(2)}, u32[]{:S(2)}) async-start(bf16[4,24,4096]{2,1,0:T(8,128)(2,1)} %reshape.303), calls=%async_computation.1 | async-start | bytes 1572864 | tf_op jit(solution)/shard_map/all_to_all | solution.py:74
  38.6 90.4 %reduce-scatter.2.cloned.1.call-start = ((), (), s32[]{:S(2)}) async-start(), calls=%async_computation.5 | async-start | bytes 3538944 | tf_op jit(solution)/shard_map/reduce_scatter | solution.py:123
  38.8 1.4 copy-start.1
  53.3 75.8 %copy-start.4 = (f32[2,192,512]{2,1,0:T(8,128)S(1)}, f32[2,192,512]{2,1,0:T(8,128)}, u32[]{:S(2)}) copy-start(f32[2,192,512]{2,1,0:T(8,128)} %param.19) | copy-start | bytes 2359300
  53.3 140.5 %all-gather.2.cloned.1.call-start = ((), (), s32[]{:S(2)}) async-start(), calls=%async_computation.6 | async-start | bytes 3538944 | tf_op jit(solution)/shard_map/all_gather | solution.py:128
  131.9 1.4 copy-start.3
  134.0 1.4 copy-start.2
  136.6 15.1 %all-to-all-start.3 = ((bf16[4,24,4096]{2,1,0:T(8,128)(2,1)}), bf16[4,24,4096]{2,1,0:T(8,128)(2,1)S(1)}, u32[]{:S(2)}, u32[]{:S(2)}) async-start(bf16[4,24,4096]{2,1,0:T(8,128)(2,1)} %bitcast.12), calls=%async_computation.3 | async-start | bytes 1572864 | tf_op jit(solution)/shard_map/all_to_all | solution.py:106
Sparse Core Ops, SparseCore 0:
  53.4 75.5 reduce-scatter.1
  132.0 61.7 all-gather.1
where the time goes:
time: 204 us; the launch traced here: 203 us
  waiting for transfers between devices  149 us (73%)
  between operations  14.9 us (7%)
  starting transfers between devices  14.8 us (7%)
  matrix products  9.41 us (5%)
  local copies, waits for them, and re-layouts  8.49 us (4%)
  other arithmetic  6.91 us (3%)
    reduce_scatter x1, waiting for transfers between devices, body(): lax.psum_scatter(cand_grads.astype(jnp.bfloat16), 'grp', scatter_dimensio...  75.7 us
    all_gather x1, waiting for transfers between devices, body(): all_dirs = lax.all_gather(dir_share, 'grp', axis=2, tiled=True)  40.3 us
    all_to_all x1, waiting for transfers between devices, body(): lax.all_to_all(partial_value.reshape(num_ep, CAP, width), 'ep', split_axi...  11.6 us
    all_to_all x1, waiting for transfers between devices, body(): lax.all_to_all(spread(send_tokens), 'ep', split_axis=0, concat_axis=0, ti...  9.85 us
    all_to_all x1, waiting for transfers between devices, body(): lax.all_to_all(spread(send_grads), 'ep', split_axis=0, concat_axis=0, til...  9.37 us
    all_to_all x1, starting transfers between devices, body(): lax.all_to_all(coeff_spread.astype(jnp.bfloat16), 'ep', split_axis=0, con...  4.24 us
  transfers between devices with their start and end apart: 6, of which 6 were waited for; matrix products, arithmetic and copies ran while one was open for 4% of the time, Pallas kernels for 0%

commit v1 on v0

--- a/solution.py
+++ b/solution.py
@@ -12,6 +12,18 @@
 adam_eps = 1e-08
 first_fix = 1.0 - math.exp(1000.0 * math.log(0.9))
 second_fix = 1.0 - math.exp(1000.0 * math.log(0.999))
+
+
+def exchange_directly(shard, axis, split, join):
+    ways, here = (lax.axis_size(axis), lax.axis_index(axis))
+    width = shard.shape[split] // ways
+    turned = jnp.roll(shard, -here * width, axis=split)
+    got = [lax.slice_in_dim(turned, 0, width, axis=split)]
+    for far in range(1, ways):
+        sent = lax.slice_in_dim(turned, far * width, (far + 1) * width, axis=split)
+        got.append(lax.ppermute(sent, axis, [(d, (d + far) % ways) for d in range(ways)]))
+    line = jnp.concatenate(got[::-1], axis=join)
+    return jnp.roll(line, (here + 1) * got[0].shape[join], axis=join)
 
 
 def moments(gradient, first_moment, second):
@@ -70,7 +82,7 @@
     w_up = up_weight[0]
     w_down = down_weight[0]
     recv_tokens, recv_grads, recv_coeffs = (
-        lax.all_to_all(spread(send_tokens), "ep", split_axis=0, concat_axis=0, tiled=True),
+        exchange_directly(spread(send_tokens), "ep", 0, 0),
         lax.all_to_all(spread(send_grads), "ep", split_axis=0, concat_axis=0, tiled=True),
         lax.all_to_all(
             coeff_spread.astype(jnp.bfloat16), "ep", split_axis=0, concat_axis=0, tiled=True

time: 204 us -> 195 us (0.956)
  waiting for transfers between devices: 149 us -> 140 us
  other arithmetic: 6.91 us -> 9.36 us
    all_to_all x1 -> x0, waiting for transfers between devices: 9.85 us -> none  [body(): lax.all_to_all(spread(send_tokens), 'ep', split_axis=0, concat_axis=0, ti...]
    all_to_all x1, waiting for transfers between devices: 1.98 us -> 5.58 us  [body(): lax.all_to_all(coeff_spread.astype(jnp.bfloat16), 'ep', split_axis=0, con...]
    all_to_all x1 -> x0, starting transfers between devices: 3.49 us -> none  [body(): lax.all_to_all(spread(send_tokens), 'ep', split_axis=0, concat_axis=0, ti...]
    ppermute x0 -> x3, starting transfers between devices: none -> 3.2 us  [exchange_directly(): lax.ppermute(sent, axis, [(d, (d + far) % ways) for d in range(ways)])]
    concatenate x0 -> x2, other arithmetic: none -> 2.44 us  [the longest x1 2.14 us: exchange_directly(): return jnp.roll(line, (here + 1) * got[0].shape[join], axis=join)]
    all_to_all x1, waiting for transfers between devices: 9.37 us -> 7.21 us  [body(): lax.all_to_all(spread(send_grads), 'ep', split_axis=0, concat_axis=0, til...]
  transfers between devices with their start and end apart: 6 -> 8, of which waited for: 6 -> 5; matrix products, arithmetic and copies ran while one was open for 4% -> 5% of each run, Pallas kernels for 0% -> 0%
where the time goes in v1:
time: 195 us
  waiting for transfers between devices  140 us (72%)
  between operations  15 us (8%)
  starting transfers between devices  13.5 us (7%)
  other arithmetic  9.36 us (5%)
  local copies, waits for them, and re-layouts  8.42 us (4%)
  matrix products  8.01 us (4%)
    reduce_scatter x1, waiting for transfers between devices, body(): lax.psum_scatter(cand_grads.astype(jnp.bfloat16), 'grp', scatter_dimensio...  75.5 us
    all_gather x1, waiting for transfers between devices, body(): all_dirs = lax.all_gather(dir_share, 'grp', axis=2, tiled=True)  40.4 us
    all_to_all x1, waiting for transfers between devices, body(): lax.all_to_all(partial_value.reshape(num_ep, CAP, width), 'ep', split_axi...  11.6 us
    all_to_all x1, waiting for transfers between devices, body(): lax.all_to_all(spread(send_grads), 'ep', split_axis=0, concat_axis=0, til...  7.21 us
    all_to_all x1, waiting for transfers between devices, body(): lax.all_to_all(coeff_spread.astype(jnp.bfloat16), 'ep', split_axis=0, con...  5.58 us
  transfers between devices with their start and end apart: 8, of which 5 were waited for; matrix products, arithmetic and copies ran while one was open for 5% of the time, Pallas kernels for 0%

profile of v1, /device:TPU:0, one launch (start us, length us, event | category | flops | bytes accessed | tf_op | source)
XLA Modules:
  0.0 194.6 jit_solution(17692581966707764759)
XLA Ops:
  7.2 0.0 copy-start
  8.0 0.7 select_reduce_fusion.1
  8.7 0.3 reduce-window.6
  9.0 0.2 slice_reduce_fusion
  9.2 0.2 reduce-window.9
  9.4 0.1 broadcast.181
  9.5 1.7 convolution_convert_fusion
  11.2 0.1 reshape.304
  11.3 0.0 copy-start.3
  11.3 0.3 fusion.21
  11.6 0.8 fusion.38
  12.4 2.4 %collective-permute-start = (bf16[1,24,4096]{2,1,0:T(8,128)(2,1)}, bf16[1,24,4096]{2,1,0:T(8,128)(2,1)}, u32[]{:S(2)}, u32[]{:S(2)}) collective-permute-start(bf16[1,24,4096]{2,1,0:T(8,128)(2,1)} %get-tuple-element.13), channel_id=1, source_target_pairs={{0,3},{1,0},{2,1},{3,2},{4,7},{5,4},{6,5},{7,6},{8,11},{9,8},{10,9... | collective-permute-start | bytes 589832 | tf_op jit(solution)/shard_map/ppermute | solution.py:24
  14.9 0.6 collective-permute-start.1
  15.4 0.2 collective-permute-start.2
  15.6 0.1 select_reduce_fusion
  15.8 0.6 reshape.302
  16.3 3.2 %all-to-all-start = ((bf16[4,1,24]{2,1,0:T(2,128)(2,1)}), bf16[4,1,24]{2,1,0:T(2,128)(2,1)S(1)}, u32[]{:S(2)}, u32[]{:S(2)}) async-start(bf16[4,1,24]{2,1,0:T(2,128)(2,1)} %reshape.302), calls=%async_computation | async-start | bytes 4096 | tf_op jit(solution)/shard_map/all_to_all | solution.py:87
  19.6 0.3 convolution_convert_fusion.1
  19.9 5.6 %all-to-all-done = bf16[4,1,24]{2,1,0:T(2,128)(2,1)S(1)} async-done(((bf16[4,1,24]{2,1,0:T(2,128)(2,1)}), bf16[4,1,24]{2,1,0:T(2,128)(2,1)S(1)}, u32[]{:S(2)}, u32[]{:S(2)}) %all-to-all-start) | async-done | bytes 224 | tf_op jit(solution)/shard_map/all_to_all | solution.py:87
  25.5 0.9 reshape.303
  26.5 3.5 %all-to-all-start.1 = ((bf16[4,24,4096]{2,1,0:T(8,128)(2,1)}), bf16[4,24,4096]{2,1,0:T(8,128)(2,1)S(1)}, u32[]{:S(2)}, u32[]{:S(2)}) async-start(bf16[4,24,4096]{2,1,0:T(8,128)(2,1)} %reshape.303), calls=%async_computation.1 | async-start | bytes 1572864 | tf_op jit(solution)/shard_map/all_to_all | solution.py:86
  30.0 0.0 reduce-scatter.2.cloned.1.call-start
  30.0 0.1 reshape.309
  30.1 2.1 %fusion.17 = bf16[4,24,4096]{2,1,0:T(8,128)(2,1)S(1)} fusion(s32[]{:T(128)S(6)} %select_n.30, bf16[1,24,4096]{2,1,0:T(8,128)(2,1)} %collective-permute-done, bf16[1,24,4096]{2,1,0:T(8,128)(2,1)} %collective-permute-done.1, bf16[1,24,4096]{2,1,0:T(8,128)(2,1)} %collective-permute-done.2, bf16[1,24,4096]{2,1,0:T(8,128)(2,1)S(1)} %get-tuple-element.10), kind=kLoop, calls=%fused_computation.36 | loop fusion | flops 2752512 | bytes 1572868 | tf_op jit(solution)/shard_map/jit(_roll_dynamic)/concatenate | solution.py:26
  32.3 0.0 copy-start.1
  32.3 0.6 fusion.5
  33.0 0.7 copy-done.1
  33.7 0.6 fusion.8
  34.4 7.2 %all-to-all-done.1 = bf16[4,24,4096]{2,1,0:T(8,128)(2,1)S(1)} async-done(((bf16[4,24,4096]{2,1,0:T(8,128)(2,1)}), bf16[4,24,4096]{2,1,0:T(8,128)(2,1)S(1)}, u32[]{:S(2)}, u32[]{:S(2)}) %all-to-all-start.1) | async-done | bytes 786464 | tf_op jit(solution)/shard_map/all_to_all | solution.py:86
  41.6 0.2 fusion.2
  41.8 0.6 fusion.23
  42.4 2.2 %multiply_convert_fusion = bf16[2,192,4096]{2,1,0:T(8,128)(2,1)} fusion(f32[192,4096]{1,0:T(8,128)S(1)} %fusion.23, f32[2]{0:T(128)S(1)} %compare_convert_fusion), kind=kLoop, calls=%fused_computation | loop fusion | flops 3145728 | bytes 6291464 | tf_op jit(solution)/shard_map/convert_element_type | solution.py:136
  44.6 0.0 reduce-scatter.2.cloned.1.call-update
  44.7 0.0 all-gather.2.cloned.1.call-start
  44.7 75.5 %reduce-scatter.2.cloned.1.call-done = bf16[2,192,512]{2,1,0:T(8,128)(2,1)} async-done(((bf16[2,192,4096]{2,1,0:T(8,128)(2,1)}), bf16[2,192,512]{2,1,0:T(8,128)(2,1)}) %reduce-scatter.2.cloned.1.call-update) | async-done | bytes 393232 | tf_op jit(solution)/shard_map/reduce_scatter | solution.py:135
  120.2 2.9 %divide_convert_fusion = (bf16[2,192,512]{2,1,0:T(8,128)(2,1)}, f32[2,192,512]{2,1,0:T(8,128)}, f32[2,192,512]{2,1,0:T(8,128)}) fusion(bf16[2,192,512]{2,1,0:T(8,128)(2,1)} %reduce-scatter.2.cloned.1.call-done, f32[2,192,512]{2,1,0:T(8,128)S(1)} %copy-done.5, f32[2,192,512]{2,1,0:T(8,128)} %param.20), kind=kLoop, calls=%fused_computation.41 | loop fusion | flops 2359296 | bytes 3932160 | tf_op jit(solution)/shard_map/convert_element_type | solution.py:139
  123.1 0.0 all-gather.2.cloned.1.call-update
  123.1 0.2 multiply_convert_fusion.1
  123.3 1.2 copy-done.4
  124.5 0.6 fusion.10
  125.2 0.4 fusion.3
  125.6 1.0 copy-done.2
  126.6 1.3 fusion.1
  127.9 3.5 %all-to-all-start.2 = ((bf16[4,24,4096]{2,1,0:T(8,128)(2,1)}), bf16[4,24,4096]{2,1,0:T(8,128)(2,1)S(1)}, u32[]{:S(2)}, u32[]{:S(2)}) async-start(bf16[4,24,4096]{2,1,0:T(8,128)(2,1)} %bitcast.12), calls=%async_computation.2 | async-start | bytes 1572864 | tf_op jit(solution)/shard_map/all_to_all | solution.py:118
  131.4 11.6 %all-to-all-done.2 = bf16[4,24,4096]{2,1,0:T(8,128)(2,1)S(1)} async-done(((bf16[4,24,4096]{2,1,0:T(8,128)(2,1)}), bf16[4,24,4096]{2,1,0:T(8,128)(2,1)S(1)}, u32[]{:S(2)}, u32[]{:S(2)}) %all-to-all-start.2) | async-done | bytes 786464 | tf_op jit(solution)/shard_map/all_to_all | solution.py:118
  143.0 1.8 fusion
  144.7 40.4 %all-gather.2.cloned.1.call-done = bf16[2,192,4096]{2,1,0:T(8,128)(2,1)} async-done(((bf16[2,192,512]{2,1,0:T(8,128)(2,1)}), bf16[2,192,4096]{2,1,0:T(8,128)(2,1)}) %all-gather.2.cloned.1.call-update) | async-done | bytes 3145744 | tf_op jit(solution)/shard_map/all_gather | solution.py:140
  185.1 2.7 %constant_dynamic-slice_fusion = bf16[1,192,4096]{2,1,0:T(8,128)(2,1)} fusion(bf16[2,192,4096]{2,1,0:T(8,128)(2,1)} %all-gather.2.cloned.1.call-done, s32[]{:T(128)S(6)} %select_n.24), kind=kLoop, calls=%fused_computation.58 | loop fusion | bytes 3145732 | tf_op jit(solution)/shard_map/jit(dynamic_index_in_dim)/dynamic_slice | solution.py:141
  (18 shorter events, 0.1 us)
Async XLA Ops:
  7.2 25.1 %copy-start = (bf16[1,4096,192]{1,2,0:T(8,128)(2,1)S(1)}, bf16[1,4096,192]{1,2,0:T(8,128)(2,1)}, u32[]{:S(2)}) copy-start(bf16[1,4096,192]{1,2,0:T(8,128)(2,1)} %param.16) | copy-start | bytes 4718596
  11.3 8.3 %copy-start.3 = (bf16[192,4096]{1,0:T(8,128)(2,1)S(1)}, bf16[192,4096]{1,0:T(8,128)(2,1)}, u32[]{:S(2)}) copy-start(bf16[192,4096]{1,0:T(8,128)(2,1)} %param.19) | copy-start | bytes 4718596
  12.4 17.7 %collective-permute-start = (bf16[1,24,4096]{2,1,0:T(8,128)(2,1)}, bf16[1,24,4096]{2,1,0:T(8,128)(2,1)}, u32[]{:S(2)}, u32[]{:S(2)}) collective-permute-start(bf16[1,24,4096]{2,1,0:T(8,128)(2,1)} %get-tuple-element.13), channel_id=1, source_target_pairs={{0,3},{1,0},{2,1},{3,2},{4,7},{5,4},{6,5},{7,6},{8,11},{9,8},{10,9... | collective-permute-start | bytes 589832 | tf_op jit(solution)/shard_map/ppermute | solution.py:24
  14.9 15.3 %collective-permute-start.1 = (bf16[1,24,4096]{2,1,0:T(8,128)(2,1)}, bf16[1,24,4096]{2,1,0:T(8,128)(2,1)}, u32[]{:S(2)}, u32[]{:S(2)}) collective-permute-start(bf16[1,24,4096]{2,1,0:T(8,128)(2,1)} %get-tuple-element.12), channel_id=1, source_target_pairs={{0,2},{1,3},{2,0},{3,1},{4,6},{5,7},{6,4},{7,5},{8,10},{9,11},{10,... | collective-permute-start | bytes 589832 | tf_op jit(solution)/shard_map/ppermute | solution.py:24
  15.4 14.7 %collective-permute-start.2 = (bf16[1,24,4096]{2,1,0:T(8,128)(2,1)}, bf16[1,24,4096]{2,1,0:T(8,128)(2,1)}, u32[]{:S(2)}, u32[]{:S(2)}) collective-permute-start(bf16[1,24,4096]{2,1,0:T(8,128)(2,1)} %get-tuple-element.11), channel_id=1, source_target_pairs={{0,1},{1,2},{2,3},{3,0},{4,5},{5,6},{6,7},{7,4},{8,9},{9,10},{10,1... | collective-permute-start | bytes 589832 | tf_op jit(solution)/shard_map/ppermute | solution.py:24
  16.3 9.2 %all-to-all-start = ((bf16[4,1,24]{2,1,0:T(2,128)(2,1)}), bf16[4,1,24]{2,1,0:T(2,128)(2,1)S(1)}, u32[]{:S(2)}, u32[]{:S(2)}) async-start(bf16[4,1,24]{2,1,0:T(2,128)(2,1)} %reshape.302), calls=%async_computation | async-start | bytes 4096 | tf_op jit(solution)/shard_map/all_to_all | solution.py:87
  26.5 15.1 %all-to-all-start.1 = ((bf16[4,24,4096]{2,1,0:T(8,128)(2,1)}), bf16[4,24,4096]{2,1,0:T(8,128)(2,1)S(1)}, u32[]{:S(2)}, u32[]{:S(2)}) async-start(bf16[4,24,4096]{2,1,0:T(8,128)(2,1)} %reshape.303), calls=%async_computation.1 | async-start | bytes 1572864 | tf_op jit(solution)/shard_map/all_to_all | solution.py:86
  30.0 90.3 %reduce-scatter.2.cloned.1.call-start = ((), (), s32[]{:S(2)}) async-start(), calls=%async_computation.4 | async-start | bytes 3538944 | tf_op jit(solution)/shard_map/reduce_scatter | solution.py:135
  32.3 1.4 copy-start.1
  44.6 75.6 %copy-start.5 = (f32[2,192,512]{2,1,0:T(8,128)S(1)}, f32[2,192,512]{2,1,0:T(8,128)}, u32[]{:S(2)}) copy-start(f32[2,192,512]{2,1,0:T(8,128)} %param.21) | copy-start | bytes 2359300
  44.7 140.4 %all-gather.2.cloned.1.call-start = ((), (), s32[]{:S(2)}) async-start(), calls=%async_computation.5 | async-start | bytes 3538944 | tf_op jit(solution)/shard_map/all_gather | solution.py:140
  123.1 1.4 copy-start.4
  125.2 1.4 copy-start.2
  127.9 15.1 %all-to-all-start.2 = ((bf16[4,24,4096]{2,1,0:T(8,128)(2,1)}), bf16[4,24,4096]{2,1,0:T(8,128)(2,1)S(1)}, u32[]{:S(2)}, u32[]{:S(2)}) async-start(bf16[4,24,4096]{2,1,0:T(8,128)(2,1)} %bitcast.12), calls=%async_computation.2 | async-start | bytes 1572864 | tf_op jit(solution)/shard_map/all_to_all | solution.py:118
Sparse Core Ops, SparseCore 0:
  44.8 75.4 reduce-scatter.1
  123.2 61.8 all-gather.1
